TPU v7x, 32 devices: a whole 2x2x4 slice. The times are simulated.
32 devices in a mesh: query: 4 (over y, x), cand: 2 (over core), tensor: 4 (over z).
Axes of the slice: x: 2, y: 2, z: 4, core: 2. Of those that a mesh axis runs over, the one named last changes fastest.
Arguments:
- cand_states: bfloat16 [8192, 2048], P(('query', 'cand'), 'tensor'), parts along dimension 0, may hold values from -6 to 6
- prefix_states: bfloat16 [256, 2048], P(('query', 'cand'), 'tensor'), parts along dimension 0, may hold values from -6 to 6
- norm_gain: float32 [2048], replicated, may hold values from 0.5 to 1.5
- w_query: bfloat16 [2048, 1024], P(None, 'tensor'), may hold values from -1 to 1
- w_key: bfloat16 [2048, 256], P(None, 'tensor'), may hold values from -1 to 1
- w_value: bfloat16 [2048, 256], P(None, 'tensor'), may hold values from -0.125 to 0.125
- w_out: bfloat16 [1024, 2048], P('tensor'), may hold values from -1.5 to 1.5
- cand_lengths: int32 [64], P(('query', 'cand')), parts along dimension 0, may hold values from 32 to 128, as said below
Outputs:
- attn_out: bfloat16 [8192, 2048], P(('query', 'cand', 'tensor')), parts along dimension 0
There are 4 independent parts, one for each index of `query`. A program takes and returns all parts, laid end to end along the dimension named above; an argument that names none is the same for every part. Nothing has to cross between parts.
Inputs may be any that keep to these rules, and one draw needn't show every extreme that they name: `cand_lengths`: some candidate has all 128 slots live.
All inputs are finite; a program needn't handle non-finite values.
Results may differ from a plain program's by a relative error of at most 0.013.
Values may be sent and summed in bfloat16 or wider, within the bound.
No kernel may reach another device: no remote copies, remote signals or barrier semaphores. Data moves between devices by JAX's collectives and lax.ppermute only.
A program may use at most 64 MiB of HBM per device.

v0:
```python
import jax
import jax.numpy as jnp
from jax import lax
from jax.sharding import PartitionSpec as P

epsilon = 1e-06
theta_base = 10000.0


def rotate(values, positions):
    half_size = values.shape[-1] // 2
    frequency = theta_base ** (-jnp.arange(half_size, dtype=jnp.float32) * 2.0 / values.shape[-1])
    angles = positions.astype(jnp.float32)[:, None] * frequency[None, :]
    cosine = jnp.cos(angles)
    sine_part = jnp.sin(angles)
    lower_half = values[:, :half_size]
    upper_half = values[:, half_size:]
    return jnp.concatenate(
        [
            lower_half * cosine - upper_half * sine_part,
            upper_half * cosine + lower_half * sine_part,
        ],
        axis=-1,
    )


def normalize(states, norm_gain):
    values = states.astype(jnp.float32)
    square = jnp.mean(values * values, axis=-1, keepdims=True)
    return (values * lax.rsqrt(square + epsilon) * norm_gain[None, :]).astype(jnp.bfloat16)


def self_scores_of(queries, cand_keys):
    scores = jnp.einsum("cqd,ckd->cqk", queries, cand_keys, preferred_element_type=jnp.float32)
    slots = jnp.arange(scores.shape[1], dtype=jnp.int32)
    causal = slots[:, None] >= slots[None, :]
    return jnp.where(causal[None], scores, -jnp.inf)


def body(cand_states, prefix_states, norm_gain, w_query, w_key, w_value, w_out, cand_lengths):
    cand_full, prefix_full = (
        lax.all_gather(cand_states, "tensor", axis=1, tiled=True),
        lax.all_gather(prefix_states, "tensor", axis=1, tiled=True),
    )
    normed_cand = normalize(cand_full, norm_gain)
    normed_prefix = normalize(prefix_full, norm_gain)
    cand_count = cand_lengths.shape[0]
    cand_len = cand_full.shape[0] // cand_count
    prefix_rows = prefix_full.shape[0]
    cand_groups = lax.axis_size("cand")
    tensor_size = lax.axis_size("tensor")
    prefix_len = prefix_rows * cand_groups
    head_size = w_query.shape[1]
    cand_pos = prefix_len + jnp.tile(jnp.arange(cand_len, dtype=jnp.int32), cand_count)
    cand_key = jnp.dot(normed_cand, w_key, preferred_element_type=jnp.float32).astype(jnp.bfloat16)
    cand_value = jnp.dot(normed_cand, w_value, preferred_element_type=jnp.float32).astype(
        jnp.bfloat16
    )
    prefix_key = jnp.dot(normed_prefix, w_key, preferred_element_type=jnp.float32).astype(
        jnp.bfloat16
    )
    prefix_value = jnp.dot(normed_prefix, w_value, preferred_element_type=jnp.float32).astype(
        jnp.bfloat16
    )
    query_rows = rotate(
        jnp.dot(normed_cand, w_query, preferred_element_type=jnp.float32), cand_pos
    ) * head_size ** (-0.5)
    queries = query_rows.astype(jnp.bfloat16).reshape(cand_count, cand_len, head_size)
    cand_key, cand_value = (
        lax.all_gather(cand_key, "tensor", axis=1, tiled=True),
        lax.all_gather(cand_value, "tensor", axis=1, tiled=True),
    )
    key_pieces, value_pieces = (
        lax.all_gather(prefix_key, ("cand", "tensor"), axis=0, tiled=True),
        lax.all_gather(prefix_value, ("cand", "tensor"), axis=0, tiled=True),
    )

    def arrange(pieces):
        blocks = pieces.reshape(cand_groups, tensor_size, prefix_rows, pieces.shape[1])
        return blocks.transpose(0, 2, 1, 3).reshape(prefix_len, pieces.shape[1] * tensor_size)

    prefix_pos = jnp.arange(prefix_len, dtype=jnp.int32)
    prefix_keys = rotate(arrange(key_pieces).astype(jnp.float32), prefix_pos).astype(jnp.bfloat16)
    prefix_values = arrange(value_pieces)
    cand_keys = (
        rotate(cand_key.astype(jnp.float32), cand_pos)
        .astype(jnp.bfloat16)
        .reshape(cand_count, cand_len, head_size)
    )
    cand_values = cand_value.reshape(cand_count, cand_len, head_size)
    self_scores = self_scores_of(queries, cand_keys)
    prefix_scores = jnp.einsum(
        "cqd,kd->cqk", queries, prefix_keys, preferred_element_type=jnp.float32
    )
    highest = jnp.maximum(self_scores.max(-1), prefix_scores.max(-1))
    self_weights = jnp.exp(self_scores - highest[..., None])
    prefix_weights = jnp.exp(prefix_scores - highest[..., None])
    divisor = self_weights.sum(-1) + prefix_weights.sum(-1)
    summed = jnp.einsum(
        "cqk,ckd->cqd",
        self_weights.astype(jnp.bfloat16),
        cand_values,
        preferred_element_type=jnp.float32,
    )
    summed = summed + jnp.einsum(
        "cqk,kd->cqd",
        prefix_weights.astype(jnp.bfloat16),
        prefix_values,
        preferred_element_type=jnp.float32,
    )
    slots = jnp.arange(cand_len, dtype=jnp.int32)
    live_rows = slots[None, :] < cand_lengths[:, None]
    head_rows = jnp.where(live_rows[..., None], summed / divisor[..., None], 0.0)
    head_rows = head_rows.reshape(cand_count * cand_len, head_size).astype(jnp.bfloat16)
    row_count = head_rows.shape[0] // tensor_size
    all_heads = lax.all_to_all(head_rows, "tensor", split_axis=0, concat_axis=1, tiled=True)
    full_out = lax.all_gather(w_out, "tensor", axis=0, tiled=True)
    summed_out = jnp.zeros((row_count, full_out.shape[1]), jnp.float32)
    for head_index in range(tensor_size):
        head_term = jnp.dot(
            all_heads[:, head_index * head_size : (head_index + 1) * head_size],
            full_out[head_index * head_size : (head_index + 1) * head_size],
            preferred_element_type=jnp.float32,
        )
        summed_out = summed_out + lax.optimization_barrier(head_term.astype(jnp.bfloat16)).astype(
            jnp.float32
        )
    return summed_out.astype(jnp.bfloat16)


def solution(mesh):
    in_specs = (
        P(("query", "cand"), "tensor"),
        P(("query", "cand"), "tensor"),
        P(),
        P(None, "tensor"),
        P(None, "tensor"),
        P(None, "tensor"),
        P("tensor", None),
        P(("query", "cand")),
    )
    out_specs = P(("query", "cand", "tensor"), None)
    return jax.shard_map(body, mesh=mesh, in_specs=in_specs, out_specs=out_specs, check_vma=False)
```

profile of v0, /device:TPU:0, one launch (start us, length us, event | category | flops | bytes accessed | tf_op | source)
XLA Modules:
  0.0 214.7 jit_solution(11699257511544938787)
XLA Ops:
  6.5 0.7 all-gather.3.cloned.1.call-update
  7.3 0.7 all-gather.5.cloned.1.call-update
  8.0 15.3 %all_gather.23 = bf16[32,2048]{1,0:T(8,128)(2,1)S(1)} all-gather(bf16[32,512]{1,0:T(8,128)(2,1)} %param.9), channel_id=1, replica_groups=mesh['query'=4,'cand'=2,'tensor'=4] {'tensor'}, dimensions={1}, use_global_device_ids=true | all-gather | bytes 163840 | tf_op jit(solution)/shard_map/all_gather | solution.py:43
  23.5 1.2 convolution_convert_fusion.7
  24.7 26.7 %all_gather.24 = bf16[256,64]{1,0:T(8,128)(2,1)S(1)} all-gather(bf16[32,64]{1,0:T(8,128)(2,1)S(1)} %convolution_convert_fusion.7), channel_id=1, replica_groups=mesh['query'=4,'cand'=2,'tensor'=4] {'cand','tensor'}, dimensions={0}, use_global_device_ids=true | all-gather | bytes 36864 | tf_op jit(solution)/shard_map/all_gather | solution.py:74
  51.6 1.2 convolution_convert_fusion.6
  52.8 27.9 %all_gather.26 = bf16[256,64]{1,0:T(8,128)(2,1)S(1)} all-gather(bf16[32,64]{1,0:T(8,128)(2,1)S(1)} %convolution_convert_fusion.6), channel_id=1, replica_groups=mesh['query'=4,'cand'=2,'tensor'=4] {'cand','tensor'}, dimensions={0}, use_global_device_ids=true | all-gather | bytes 36864 | tf_op jit(solution)/shard_map/all_gather | solution.py:75
  81.3 13.3 %all-gather.3.cloned.1.call-done = bf16[1024,2048]{1,0:T(8,128)(2,1)} async-done(((bf16[1024,512]{1,0:T(8,128)(2,1)}), bf16[1024,2048]{1,0:T(8,128)(2,1)}) %all-gather.3.cloned.1.call-update) | async-done | bytes 4194320 | tf_op jit(solution)/shard_map/all_gather | solution.py:42
  94.6 3.2 %fusion = f32[1024]{0:T(1024)S(1)} fusion(bf16[1024,2048]{1,0:T(8,128)(2,1)} %all-gather.3.cloned.1.call-done), kind=kLoop, calls=%fused_computation.2 | loop fusion | flops 6290432 | bytes 4198400 | tf_op jit(solution)/shard_map/reduce_sum | solution.py:29
  98.0 1.0 fusion.2
  99.1 2.0 copy-done.1
  101.0 1.4 convolution_convert_fusion.5
  102.4 21.4 %all_gather.22 = bf16[1024,256]{0,1:T(8,128)(2,1)S(1)} all-gather(bf16[1024,64]{0,1:T(8,128)(2,1)S(1)} %convolution_convert_fusion.5), channel_id=1, replica_groups=mesh['query'=4,'cand'=2,'tensor'=4] {'tensor'}, dimensions={1}, use_global_device_ids=true | all-gather | bytes 655360 | tf_op jit(solution)/shard_map/all_gather | solution.py:70
  124.1 3.6 %convolution_convert_fusion.4 = bf16[1024,64]{0,1:T(8,128)(2,1)S(1)} fusion(bf16[1024,2048]{1,0:T(8,128)(2,1)} %copy-done.1, bf16[2048,64]{0,1:T(8,128)(2,1)S(1)} %copy-done.5), kind=kOutput, calls=%fused_computation.15 | convolution fusion | flops 268500992 | bytes 4587520 | tf_op jit(solution)/shard_map/dot_general | solution.py:56
  127.7 21.3 %all_gather.25 = bf16[1024,256]{0,1:T(8,128)(2,1)S(1)} all-gather(bf16[1024,64]{0,1:T(8,128)(2,1)S(1)} %convolution_convert_fusion.4), channel_id=1, replica_groups=mesh['query'=4,'cand'=2,'tensor'=4] {'tensor'}, dimensions={1}, use_global_device_ids=true | all-gather | bytes 655360 | tf_op jit(solution)/shard_map/all_gather | solution.py:71
  149.2 3.5 %fusion.67 = f32[1024,256]{1,0:T(8,128)S(1)} fusion(bf16[1024,2048]{1,0:T(8,128)(2,1)} %copy-done.1, bf16[2048,256]{1,0:T(8,128)(2,1)S(1)} %copy-done), kind=kOutput, calls=%fused_computation.92 | convolution fusion | flops 1073741824 | bytes 6291456 | tf_op jit(solution)/shard_map/dot_general | solution.py:66
  152.7 2.5 %fusion.19 = (f32[1024,128]{1,0:T(8,128)S(1)}, f32[1024,128]{1,0:T(8,128)S(1)}, bf16[1024,128]{1,0:T(8,128)(2,1)S(1)}, bf16[1024,128]{1,0:T(8,128)(2,1)S(1)}) fusion(f32[1024,256]{1,0:T(8,128)S(1)} %fusion.67, f32[128]{0:T(128)S(1)} %multiply_power_fusion, f32[1024]{0:T(1024)S(1)} %convert_bitcast_fusion.1, f32[1024,256]{1,0:T(8,128)S(1)} %convert_element_type.144), kind=kLoop, calls=%fused_computation.35 | loop fusion | flops 1966080 | bytes 3674624 | tf_op jit(solution)/shard_map/sub | solution.py:20
  156.8 1.0 copy.25
  157.8 5.3 %all-to-all-start = ((bf16[4,256,256]{1,2,0:T(8,128)(2,1)}), bf16[4,256,256]{1,2,0:T(8,128)(2,1)S(1)}, u32[]{:S(2)}, u32[]{:S(2)}) async-start(bf16[4,256,256]{1,2,0:T(8,128)(2,1)} %copy.25), calls=%async_computation | async-start | bytes 1048576 | tf_op jit(solution)/shard_map/all_to_all | solution.py:116
  163.1 38.6 %all-gather.5.cloned.1.call-done = bf16[1024,2048]{1,0:T(8,128)(2,1)} async-done(((bf16[256,2048]{1,0:T(8,128)(2,1)}), bf16[1024,2048]{1,0:T(8,128)(2,1)}) %all-gather.5.cloned.1.call-update) | async-done | bytes 4194320 | tf_op jit(solution)/shard_map/all_gather | solution.py:117
  201.7 1.8 convolution_convert_fusion.3
  203.6 1.7 convolution_convert_fusion.2
  205.3 0.5 convolution_convert_fusion.1
  206.2 1.7 add_convert_fusion
  (44 shorter events, 3.6 us)
Async XLA Ops:
  6.5 142.7 %copy-start = (bf16[2048,256]{1,0:T(8,128)(2,1)S(1)}, bf16[2048,256]{1,0:T(8,128)(2,1)}, u32[]{:S(2)}) copy-start(bf16[2048,256]{1,0:T(8,128)(2,1)} %param.11) | copy-start | bytes 3145732
  6.5 91.3 %copy-start.6 = (f32[2048]{0:T(1024)S(1)}, f32[2048]{0:T(1024)}, u32[]{:S(2)}) copy-start(f32[2048]{0:T(1024)} %param.10) | copy-start | bytes 24580
  6.5 74.5 %copy-start.7 = (s32[8]{0:T(128)S(1)}, s32[8]{0:T(128)}, u32[]{:S(2)}) copy-start(s32[8]{0:T(128)} %param.15) | copy-start | bytes 100
  6.5 88.0 %all-gather.3.cloned.1.call-start = ((), (), s32[]{:S(2)}) async-start(), calls=%async_computation.1 | async-start | bytes 5242880 | tf_op jit(solution)/shard_map/all_gather | solution.py:42
  7.3 194.5 %all-gather.5.cloned.1.call-start = ((), (), s32[]{:S(2)}) async-start(), calls=%async_computation.2 | async-start | bytes 5242880 | tf_op jit(solution)/shard_map/all_gather | solution.py:117
  94.6 3.4 %copy-start.2 = (bf16[1024,2048]{1,0:T(8,128)(2,1)S(1)}, bf16[1024,2048]{1,0:T(8,128)(2,1)}, u32[]{:S(2)}) copy-start(bf16[1024,2048]{1,0:T(8,128)(2,1)} %all-gather.3.cloned.1.call-done) | copy-start | bytes 12582916
  98.0 3.0 %copy-start.4 = (bf16[2048,64]{0,1:T(8,128)(2,1)S(1)}, bf16[2048,64]{0,1:T(8,128)(2,1)}, u32[]{:S(2)}) copy-start(bf16[2048,64]{0,1:T(8,128)(2,1)} %param.12) | copy-start | bytes 786436
  99.0 2.0 copy-start.1
  101.0 23.0 %copy-start.5 = (bf16[2048,64]{0,1:T(8,128)(2,1)S(1)}, bf16[2048,64]{0,1:T(8,128)(2,1)}, u32[]{:S(2)}) copy-start(bf16[2048,64]{0,1:T(8,128)(2,1)} %param.13) | copy-start | bytes 786436
  157.8 44.0 %all-to-all-start = ((bf16[4,256,256]{1,2,0:T(8,128)(2,1)}), bf16[4,256,256]{1,2,0:T(8,128)(2,1)S(1)}, u32[]{:S(2)}, u32[]{:S(2)}) async-start(bf16[4,256,256]{1,2,0:T(8,128)(2,1)} %copy.25), calls=%async_computation | async-start | bytes 1048576 | tf_op jit(solution)/shard_map/all_to_all | solution.py:116
  201.7 3.5 %copy-start.3 = (bf16[1024,2048]{1,0:T(8,128)(2,1)S(1)}, bf16[1024,2048]{1,0:T(8,128)(2,1)}, u32[]{:S(2)}) copy-start(bf16[1024,2048]{1,0:T(8,128)(2,1)} %all-gather.5.cloned.1.call-done) | copy-start | bytes 12582916
Sparse Core Ops, SparseCore 0:
  8.9 85.6 all-gather.2
  96.1 105.5 all-gather.4
where the time goes:
time: 215 us
  blocking collectives  113 us (53%)
  waiting for transfers between devices  53.3 us (25%)
  matrix products  16.8 us (8%)
  between operations  13.6 us (6%)
  other arithmetic  9.09 us (4%)
  starting transfers between devices  5.36 us (2%)
  local copies, waits for them, and re-layouts  3.97 us (2%)
    all_gather x1, waiting for transfers between devices, body(): full_out = lax.all_gather(w_out, 'tensor', axis=0, tiled=True)  38.6 us
    all_gather x1, blocking collectives, body(): lax.all_gather(prefix_value, ('cand', 'tensor'), axis=0, tiled=True)  27.9 us
    all_gather x1, blocking collectives, body(): lax.all_gather(prefix_key, ('cand', 'tensor'), axis=0, tiled=True)  26.7 us
    all_gather x1, blocking collectives, body(): lax.all_gather(cand_key, 'tensor', axis=1, tiled=True)  21.4 us
    all_gather x1, blocking collectives, body(): lax.all_gather(cand_value, 'tensor', axis=1, tiled=True)  21.3 us
    all_gather x1, blocking collectives, body(): lax.all_gather(prefix_states, 'tensor', axis=1, tiled=True)  15.3 us
    all_gather x1, waiting for transfers between devices, body(): lax.all_gather(cand_states, 'tensor', axis=1, tiled=True)  13.3 us
    all_to_all x1, starting transfers between devices, body(): lax.all_to_all(head_rows, 'tensor', split_axis=0, concat_axis=1, tiled=True)  5.32 us
  transfers between devices with their start and end apart: 3, of which 2 were waited for; matrix products, arithmetic and copies ran while one was open for 10% of the time, Pallas kernels for 0%

commit v1 on v0

--- a/solution.py
+++ b/solution.py
@@ -114,7 +114,14 @@
     head_rows = head_rows.reshape(cand_count * cand_len, head_size).astype(jnp.bfloat16)
     row_count = head_rows.shape[0] // tensor_size
     all_heads = lax.all_to_all(head_rows, "tensor", split_axis=0, concat_axis=1, tiled=True)
-    full_out = lax.all_gather(w_out, "tensor", axis=0, tiled=True)
+    ring = [w_out]
+    for hop in range(3):
+        ring.append(lax.ppermute(ring[-1], "tensor", [(dev, (dev + 1) % 4) for dev in range(4)]))
+    full_out = jnp.roll(
+        jnp.concatenate(ring[::-1], axis=0),
+        (lax.axis_index("tensor") + 1) * ring[0].shape[0],
+        axis=0,
+    )
     summed_out = jnp.zeros((row_count, full_out.shape[1]), jnp.float32)
     for head_index in range(tensor_size):
         head_term = jnp.dot(

time: 215 us -> 305 us (1.42)
  blocking collectives: 113 us -> 169 us
  starting transfers between devices: 5.36 us -> 23.8 us
  local copies, waits for them, and re-layouts: 3.97 us -> 20.9 us
  waiting for transfers between devices: 53.3 us -> 42 us
  other arithmetic: 9.09 us -> 15.4 us
    all_gather x1, blocking collectives: 15.3 us -> 69.7 us  [body(): lax.all_gather(prefix_states, 'tensor', axis=1, tiled=True)]
    all_gather x1 -> x0, waiting for transfers between devices: 38.6 us -> none  [body(): full_out = lax.all_gather(w_out, 'tensor', axis=0, tiled=True)]
    ppermute x0 -> x3, waiting for transfers between devices: none -> 37.6 us  [body(): lax.ppermute(ring[-1], 'tensor', [(dev, (dev + 1) % 4) for dev in range(4)])]
    ppermute x0 -> x3, starting transfers between devices: none -> 19.5 us  [body(): lax.ppermute(ring[-1], 'tensor', [(dev, (dev + 1) % 4) for dev in range(4)])]
    all_gather x1, blocking collectives: 27.9 us -> 42.9 us  [body(): lax.all_gather(prefix_value, ('cand', 'tensor'), axis=0, tiled=True)]
    all_gather x1, waiting for transfers between devices: 13.3 us -> 0.01 us  [body(): lax.all_gather(cand_states, 'tensor', axis=1, tiled=True)]
    unnamed x16 -> x25, local copies, waits for them, and re-layouts: 2.19 us -> 13.2 us
    all_gather x1, blocking collectives: 21.4 us -> 15.7 us  [body(): lax.all_gather(cand_key, 'tensor', axis=1, tiled=True)]
  transfers between devices with their start and end apart: 3 -> 5, of which waited for: 2 -> 2; matrix products, arithmetic and copies ran while one was open for 10% -> 6% of each run, Pallas kernels for 0% -> 0%
where the time goes in v1:
time: 305 us; the launch traced here: 304 us
  blocking collectives  169 us (55%)
  waiting for transfers between devices  42 us (14%)
  starting transfers between devices  23.8 us (8%)
  local copies, waits for them, and re-layouts  20.9 us (7%)
  matrix products  18.9 us (6%)
  other arithmetic  15.4 us (5%)
  between operations  13.6 us (4%)
    all_gather x1, blocking collectives, body(): lax.all_gather(prefix_states, 'tensor', axis=1, tiled=True)  69.7 us
    all_gather x1, blocking collectives, body(): lax.all_gather(prefix_value, ('cand', 'tensor'), axis=0, tiled=True)  42.9 us
    ppermute x3, waiting for transfers between devices, body(): lax.ppermute(ring[-1], 'tensor', [(dev, (dev + 1) % 4) for dev in range(4)])  37.6 us
    all_gather x1, blocking collectives, body(): lax.all_gather(prefix_key, ('cand', 'tensor'), axis=0, tiled=True)  23.8 us
    ppermute x3, starting transfers between devices, body(): lax.ppermute(ring[-1], 'tensor', [(dev, (dev + 1) % 4) for dev in range(4)])  19.5 us
    all_gather x1, blocking collectives, body(): lax.all_gather(cand_value, 'tensor', axis=1, tiled=True)  17 us
    all_gather x1, blocking collectives, body(): lax.all_gather(cand_key, 'tensor', axis=1, tiled=True)  15.7 us
    unnamed x25, local copies, waits for them, and re-layouts  13.2 us
  transfers between devices with their start and end apart: 5, of which 2 were waited for; matrix products, arithmetic and copies ran while one was open for 6% of the time, Pallas kernels for 0%

profile of v1, /device:TPU:0, one launch (start us, length us, event | category | flops | bytes accessed | tf_op | source)
XLA Modules:
  0.0 303.9 jit_solution(13000517315887828273)
XLA Ops:
  7.3 3.1 %collective-permute-start = (bf16[256,2048]{1,0:T(8,128)(2,1)}, bf16[256,2048]{1,0:T(8,128)(2,1)S(1)}, u32[]{:S(2)}, u32[]{:S(2)}) collective-permute-start(bf16[256,2048]{1,0:T(8,128)(2,1)} %param.14), channel_id=1, source_target_pairs={{0,1},{1,2},{2,3},{3,0},{4,5},{5,6},{6,7},{7,4},{8,9},{9,10},{10,1... | collective-permute-start | bytes 3145736 | tf_op jit(solution)/shard_map/ppermute | solution.py:119
  10.4 37.6 %collective-permute-done = bf16[256,2048]{1,0:T(8,128)(2,1)S(1)} collective-permute-done((bf16[256,2048]{1,0:T(8,128)(2,1)}, bf16[256,2048]{1,0:T(8,128)(2,1)S(1)}, u32[]{:S(2)}, u32[]{:S(2)}) %collective-permute-start) | collective-permute-done | bytes 1048608 | tf_op jit(solution)/shard_map/ppermute | solution.py:119
  47.9 14.7 %collective-permute-start.1 = (bf16[256,2048]{1,0:T(8,128)(2,1)S(1)}, bf16[256,2048]{1,0:T(8,128)(2,1)}, u32[]{:S(2)}, u32[]{:S(2)}) collective-permute-start(bf16[256,2048]{1,0:T(8,128)(2,1)S(1)} %collective-permute-done), channel_id=1, source_target_pairs={{0,1},{1,2},{2,3},{3,0},{4,5},{5,6},{6,7},{7,4},{8,9},{9,10},{10,1... | collective-permute-start | bytes 3145736 | tf_op jit(solution)/shard_map/ppermute | solution.py:119
  62.7 69.7 %all_gather.20 = bf16[32,2048]{1,0:T(8,128)(2,1)S(1)} all-gather(bf16[32,512]{1,0:T(8,128)(2,1)} %param.9), channel_id=1, replica_groups=mesh['query'=4,'cand'=2,'tensor'=4] {'tensor'}, dimensions={1}, use_global_device_ids=true | all-gather | bytes 163840 | tf_op jit(solution)/shard_map/all_gather | solution.py:43
  133.8 23.8 %all_gather.21 = bf16[256,64]{1,0:T(8,128)(2,1)S(1)} all-gather(bf16[32,64]{1,0:T(8,128)(2,1)S(1)} %convolution_convert_fusion.7), channel_id=1, replica_groups=mesh['query'=4,'cand'=2,'tensor'=4] {'cand','tensor'}, dimensions={0}, use_global_device_ids=true | all-gather | bytes 36864 | tf_op jit(solution)/shard_map/all_gather | solution.py:74
  160.7 42.9 %all_gather.23 = bf16[256,64]{1,0:T(8,128)(2,1)S(1)} all-gather(bf16[32,64]{1,0:T(8,128)(2,1)S(1)} %convolution_convert_fusion.6), channel_id=1, replica_groups=mesh['query'=4,'cand'=2,'tensor'=4] {'cand','tensor'}, dimensions={0}, use_global_device_ids=true | all-gather | bytes 36864 | tf_op jit(solution)/shard_map/all_gather | solution.py:75
  206.0 2.3 constant_dynamic-update-slice_fusion.7
  208.3 2.3 constant_dynamic-update-slice_fusion.6
  212.8 3.1 %fusion = f32[1024]{0:T(1024)S(1)} fusion(bf16[1024,2048]{1,0:T(8,128)(2,1)} %all-gather.2.cloned.1.call-done), kind=kLoop, calls=%fused_computation.2 | loop fusion | flops 6290432 | bytes 4198400 | tf_op jit(solution)/shard_map/reduce_sum | solution.py:29
  216.0 3.2 %fusion.2 = bf16[1024,2048]{1,0:T(8,128)(2,1)S(1)} fusion(bf16[1024,2048]{1,0:T(8,128)(2,1)} %all-gather.2.cloned.1.call-done, f32[2048]{0:T(1024)S(1)} %copy-done.7, f32[1024]{0:T(1024)S(1)} %add_rsqrt_fusion), kind=kLoop, calls=%fused_computation.4 | loop fusion | flops 8388608 | bytes 8400896 | tf_op jit(solution)/shard_map/convert_element_type | solution.py:30
  222.5 17.0 %all_gather.22 = bf16[1024,256]{0,1:T(8,128)(2,1)} all-gather(bf16[1024,64]{0,1:T(8,128)(2,1)S(1)} %convolution_convert_fusion.4), channel_id=1, replica_groups=mesh['query'=4,'cand'=2,'tensor'=4] {'tensor'}, dimensions={1}, use_global_device_ids=true | all-gather | bytes 655360 | tf_op jit(solution)/shard_map/all_gather | solution.py:71
  239.6 2.1 copy.27
  241.7 4.4 %fusion.71 = f32[1024,256]{1,0:T(8,128)} fusion(bf16[1024,2048]{1,0:T(8,128)(2,1)} %copy-done.1, bf16[2048,256]{1,0:T(8,128)(2,1)S(1)} %copy-done), kind=kOutput, calls=%fused_computation.104 | convolution fusion | flops 1073741824 | bytes 6291456 | tf_op jit(solution)/shard_map/dot_general | solution.py:66
  246.1 15.7 %all_gather.19 = bf16[1024,256]{0,1:T(8,128)(2,1)} all-gather(bf16[1024,64]{0,1:T(8,128)(2,1)S(1)} %convolution_convert_fusion.5), channel_id=1, replica_groups=mesh['query'=4,'cand'=2,'tensor'=4] {'tensor'}, dimensions={1}, use_global_device_ids=true | all-gather | bytes 655360 | tf_op jit(solution)/shard_map/all_gather | solution.py:70
  261.8 2.1 copy.20
  265.1 3.8 %fusion.19 = (f32[1024,128]{1,0:T(8,128)S(1)}, f32[1024,128]{1,0:T(8,128)S(1)}, bf16[1024,128]{1,0:T(8,128)(2,1)S(1)}, bf16[1024,128]{1,0:T(8,128)(2,1)S(1)}) fusion(f32[1024,256]{1,0:T(8,128)} %fusion.71, f32[128]{0:T(128)S(1)} %multiply_power_fusion, f32[1024]{0:T(1024)S(1)} %convert_bitcast_fusion.1, f32[1024,256]{1,0:T(8,128)S(1)} %convert_element_type.144), kind=kLoop, calls=%fused_computation.35 | loop fusion | flops 1966080 | bytes 3674624 | tf_op jit(solution)/shard_map/sub | solution.py:20
  271.3 2.1 copy.25
  273.4 4.3 %all-to-all-start = ((bf16[4,256,256]{1,2,0:T(8,128)(2,1)}), bf16[4,256,256]{1,2,0:T(8,128)(2,1)}, u32[]{:S(2)}, u32[]{:S(2)}) async-start(bf16[4,256,256]{1,2,0:T(8,128)(2,1)} %copy.25), calls=%async_computation | async-start | bytes 1048576 | tf_op jit(solution)/shard_map/all_to_all | solution.py:116
  277.8 2.3 constant_dynamic-update-slice_fusion.3
  280.1 2.3 constant_dynamic-update-slice_fusion.2
  284.6 3.7 %all-to-all-done = bf16[4,256,256]{1,2,0:T(8,128)(2,1)} async-done(((bf16[4,256,256]{1,2,0:T(8,128)(2,1)}), bf16[4,256,256]{1,2,0:T(8,128)(2,1)}, u32[]{:S(2)}, u32[]{:S(2)}) %all-to-all-start) | async-done | bytes 524320 | tf_op jit(solution)/shard_map/all_to_all | solution.py:116
  290.1 1.8 convolution_convert_fusion
  291.8 1.8 convolution_convert_fusion.1
  293.6 1.8 convolution_convert_fusion.2
  (57 shorter events, 22.2 us)
Async XLA Ops:
  6.5 235.1 %copy-start = (bf16[2048,256]{1,0:T(8,128)(2,1)S(1)}, bf16[2048,256]{1,0:T(8,128)(2,1)}, u32[]{:S(2)}) copy-start(bf16[2048,256]{1,0:T(8,128)(2,1)} %param.11) | copy-start | bytes 3145732
  6.5 205.2 %copy-start.2 = (bf16[256,2048]{1,0:T(8,128)(2,1)S(1)}, bf16[256,2048]{1,0:T(8,128)(2,1)}, u32[]{:S(2)}) copy-start(bf16[256,2048]{1,0:T(8,128)(2,1)} %param.14) | copy-start | bytes 3145732
  6.5 209.4 %copy-start.7 = (f32[2048]{0:T(1024)S(1)}, f32[2048]{0:T(1024)}, u32[]{:S(2)}) copy-start(f32[2048]{0:T(1024)} %param.10) | copy-start | bytes 24580
  6.5 206.3 %all-gather.2.cloned.1.call-start = ((), (), s32[]{:S(2)}) async-start(), calls=%async_computation.1 | async-start | bytes 5242880 | tf_op jit(solution)/shard_map/all_gather | solution.py:42
  7.3 40.7 %collective-permute-start = (bf16[256,2048]{1,0:T(8,128)(2,1)}, bf16[256,2048]{1,0:T(8,128)(2,1)S(1)}, u32[]{:S(2)}, u32[]{:S(2)}) collective-permute-start(bf16[256,2048]{1,0:T(8,128)(2,1)} %param.14), channel_id=1, source_target_pairs={{0,1},{1,2},{2,3},{3,0},{4,5},{5,6},{6,7},{7,4},{8,9},{9,10},{10,1... | collective-permute-start | bytes 3145736 | tf_op jit(solution)/shard_map/ppermute | solution.py:119
  47.9 109.9 %collective-permute-start.1 = (bf16[256,2048]{1,0:T(8,128)(2,1)S(1)}, bf16[256,2048]{1,0:T(8,128)(2,1)}, u32[]{:S(2)}, u32[]{:S(2)}) collective-permute-start(bf16[256,2048]{1,0:T(8,128)(2,1)S(1)} %collective-permute-done), channel_id=1, source_target_pairs={{0,1},{1,2},{2,3},{3,0},{4,5},{5,6},{6,7},{7,4},{8,9},{9,10},{10,1... | collective-permute-start | bytes 3145736 | tf_op jit(solution)/shard_map/ppermute | solution.py:119
  157.9 48.1 %collective-permute-start.2 = (bf16[256,2048]{1,0:T(8,128)(2,1)}, bf16[256,2048]{1,0:T(8,128)(2,1)}, u32[]{:S(2)}, u32[]{:S(2)}) collective-permute-start(bf16[256,2048]{1,0:T(8,128)(2,1)} %collective-permute-done.1), channel_id=1, source_target_pairs={{0,1},{1,2},{2,3},{3,0},{4,5},{5,6},{6,7},{7,4},{8,9},{9,10},{10,1... | collective-permute-start | bytes 3145736 | tf_op jit(solution)/shard_map/ppermute | solution.py:119
  210.6 8.6 %copy-start.4 = (bf16[2048,64]{0,1:T(8,128)(2,1)S(1)}, bf16[2048,64]{0,1:T(8,128)(2,1)}, u32[]{:S(2)}) copy-start(bf16[2048,64]{0,1:T(8,128)(2,1)} %param.13) | copy-start | bytes 786436
  212.8 8.3 %copy-start.5 = (bf16[2048,64]{0,1:T(8,128)(2,1)S(1)}, bf16[2048,64]{0,1:T(8,128)(2,1)}, u32[]{:S(2)}) copy-start(bf16[2048,64]{0,1:T(8,128)(2,1)} %param.12) | copy-start | bytes 786436
  219.2 1.9 copy-start.1
  239.6 29.6 %copy-start.6 = (pred[128,128]{0,1:T(8,128)(4,1)S(1)}, pred[128,128]{0,1:T(8,128)(4,1)}, u32[]{:S(2)}) copy-start(pred[128,128]{0,1:T(8,128)(4,1)} %iota_compare_fusion) | copy-start | bytes 49156
  246.1 24.0 %copy-start.8 = (pred[8,128]{1,0:T(8,128)(4,1)S(1)}, pred[8,128]{1,0:T(8,128)(4,1)}, u32[]{:S(2)}) copy-start(pred[8,128]{1,0:T(8,128)(4,1)} %iota_compare_fusion.1) | copy-start | bytes 3076
  263.9 5.8 %copy-start.3 = (bf16[1024,256]{1,0:T(8,128)(2,1)S(1)}, bf16[1024,256]{1,0:T(8,128)(2,1)}, u32[]{:S(2)}) copy-start(bf16[1024,256]{1,0:T(8,128)(2,1)} %copy.27) | copy-start | bytes 1572868
  273.4 14.9 %all-to-all-start = ((bf16[4,256,256]{1,2,0:T(8,128)(2,1)}), bf16[4,256,256]{1,2,0:T(8,128)(2,1)}, u32[]{:S(2)}, u32[]{:S(2)}) async-start(bf16[4,256,256]{1,2,0:T(8,128)(2,1)} %copy.25), calls=%async_computation | async-start | bytes 1048576 | tf_op jit(solution)/shard_map/all_to_all | solution.py:116
Sparse Core Ops, SparseCore 0:
  8.9 118.1 all-gather.1
